TPU v7x, 256 devices: a whole 4x4x8 slice. The times are simulated.
256 devices in a mesh: seq: 16 (over y_lo, z), dp: 16 (over x, y_hi, core).
Axes of the slice: x: 4, y: 4 (y_hi: 2, y_lo: 2; y = y_hi * 2 + y_lo), z: 8, core: 2. Of those that a mesh axis runs over, the one named last changes fastest.
Arguments:
- layer_rows: bfloat16 [16, 2048, 1024], P('dp', 'seq'), may hold values from -6 to 6
- doc_ids: int32 [16, 2048], P('dp', 'seq'), may hold values from 0 to 5, never falling along the last dimension, each value on 1 to 1024 neighbouring positions
- packing: int32 [16, 16], P('dp'), may hold values from 0 to 15, each once within a row
- norm_gain: float32 [1024], replicated, may hold values from 0.1 to 1.9
- w_qkv: bfloat16 [1024, 3072], replicated, may hold values from -0.1875 to 0.1875
- d_attn: bfloat16 [16, 2048, 1024], P('dp', 'seq'), may hold values from -6 to 6
Outputs:
- d_input: bfloat16 [16, 2048, 1024], P('dp', 'seq')
- w_grad: float32 [1024, 3072], P('seq')
Inputs may be any that keep to these rules, and one draw needn't show every extreme that they name: `doc_ids`: in each group the song numbers never fall along the initial order; every number occurs, and one song spans exactly 1024 frames. `packing`: each group's row names every block number once.
All inputs are finite; a program needn't handle non-finite values.
Results may differ from a plain program's by a relative error of at most 0.024.
Values may be sent and summed in bfloat16 or wider, within the bound.
No kernel may reach another device: no remote copies, remote signals or barrier semaphores. Data moves between devices by JAX's collectives and lax.ppermute only.
A program may use at most 128 MiB of HBM per device.

v0:
```python
import math
import jax
import jax.numpy as jnp
from jax import lax
from jax.sharding import PartitionSpec as P

HEADS = 8
HEAD = 128
BLOCK = 128


def rounded(value):
    return lax.optimization_barrier(value.astype(jnp.bfloat16)).astype(jnp.float32)


def normalize(frames, norm_gain):
    values = frames.astype(jnp.float32)
    inverse = lax.rsqrt(jnp.mean(values * values, axis=-1, keepdims=True) + 1e-05)
    unit_rows = values * inverse
    return (inverse, unit_rows, (unit_rows * norm_gain).astype(jnp.bfloat16))


def body(layer_rows, doc_ids, packing, norm_gain, w_qkv, d_attn):
    shards = lax.axis_size("seq")
    my_index = lax.axis_index("seq")
    frames = layer_rows[0]
    tok_rows = frames.shape[0]
    head_cols = HEADS * HEAD
    total_keys = tok_rows * shards
    block_order = packing[0]
    key_pos = (block_order[:, None] * BLOCK + jnp.arange(BLOCK, dtype=jnp.int32)[None, :]).reshape(
        total_keys
    )
    first_own = my_index * tok_rows
    my_pos = lax.dynamic_slice_in_dim(key_pos, first_own, tok_rows, 0)
    doc_low = doc_ids[0].astype(jnp.bfloat16)
    pieces = (
        lax.all_gather(frames, "seq", axis=0, tiled=True),
        lax.all_gather(doc_low, "seq", axis=0, tiled=True),
    )
    length = pieces[0].shape[0]
    inside = (my_pos >= 0) & (my_pos < length)
    clipped = jnp.clip(my_pos, 0, length - 1)
    new_rows = jnp.where(
        inside[:, None], jnp.take(pieces[0], clipped, axis=0), jnp.zeros_like(frames)
    )
    new_docs = jnp.where(inside, jnp.take(pieces[1], clipped, axis=0), jnp.zeros_like(doc_low))
    inverse, unit_rows, normed = normalize(new_rows, norm_gain)
    projected = jnp.dot(normed, w_qkv, preferred_element_type=jnp.float32).astype(jnp.bfloat16)
    queries = projected[:, :head_cols]
    all_keys, all_values, key_docs_low = (
        lax.all_gather(projected[:, head_cols : 2 * head_cols], "seq", axis=0, tiled=True),
        lax.all_gather(projected[:, 2 * head_cols :], "seq", axis=0, tiled=True),
        lax.all_gather(new_docs, "seq", axis=0, tiled=True),
    )
    key_docs = key_docs_low.astype(jnp.int32)
    my_docs = lax.dynamic_slice_in_dim(key_docs, first_own, tok_rows, 0)
    factor = 1.0 / math.sqrt(HEAD)
    q_heads = queries.reshape(tok_rows, HEADS, HEAD)
    grad_heads = d_attn[0].reshape(tok_rows, HEADS, HEAD)
    group_count = total_keys // total_keys

    def key_slab(group_idx):
        first_key = group_idx * total_keys
        slab_keys = all_keys.reshape(total_keys, HEADS, HEAD)
        slab_values = all_values.reshape(total_keys, HEADS, HEAD)
        allowed = (my_docs[:, None] == key_docs[None, :]) & (key_pos[None, :] <= my_pos[:, None])
        return (first_key, slab_keys, slab_values, allowed)

    def exp_scores(query_part, slab_keys, allowed):
        scores = (
            jnp.einsum("qhd,khd->hqk", query_part, slab_keys, preferred_element_type=jnp.float32)
            * factor
        )
        return jnp.where(allowed[None], jnp.exp(scores), jnp.float32(0.0))

    def add_denominator(group_idx, running):
        first_key, slab_keys, slab_values, allowed = key_slab(group_idx)
        return running + jnp.sum(exp_scores(q_heads, slab_keys, allowed), axis=-1)

    denominator = lax.fori_loop(
        0, group_count, add_denominator, jnp.zeros((HEADS, tok_rows), jnp.float32)
    )

    def probabilities(slab_keys, allowed):
        attn_prob = exp_scores(q_heads, slab_keys, allowed) / denominator[:, :, None]
        return (attn_prob, attn_prob.astype(jnp.bfloat16))

    def add_output(group_idx, running):
        first_key, slab_keys, slab_values, allowed = key_slab(group_idx)

        def compute():
            attn_prob, prob_low = probabilities(slab_keys, allowed)
            return jnp.einsum(
                "hqk,khd->qhd", prob_low, slab_values, preferred_element_type=jnp.float32
            )

        return running + compute()

    outputs = lax.fori_loop(
        0, group_count, add_output, jnp.zeros((tok_rows, HEADS, HEAD), jnp.float32)
    )
    row_delta = jnp.sum(grad_heads.astype(jnp.float32) * outputs, axis=-1).T

    def slab_backward(slab_keys, slab_values, allowed):
        attn_prob, prob_low = probabilities(slab_keys, allowed)
        grad_prob = jnp.einsum(
            "qhd,khd->hqk", grad_heads, slab_values, preferred_element_type=jnp.float32
        )
        dscore = (attn_prob * (grad_prob - row_delta[:, :, None])).astype(jnp.bfloat16)
        dq_part = (
            jnp.einsum("hqk,khd->qhd", dscore, slab_keys, preferred_element_type=jnp.float32)
            * factor
        )
        return (dq_part, dscore, prob_low)

    def add_grads(group_idx, running):
        dq_sum, kv_grads = running
        first_key, slab_keys, slab_values, allowed = key_slab(group_idx)

        def compute():
            dq_part, dscore, prob_low = slab_backward(slab_keys, slab_values, allowed)
            dk_part = (
                jnp.einsum("hqk,qhd->khd", dscore, q_heads, preferred_element_type=jnp.float32)
                * factor
            )
            dv_part = jnp.einsum(
                "hqk,qhd->khd", prob_low, grad_heads, preferred_element_type=jnp.float32
            )
            return (
                dq_part,
                jnp.concatenate(
                    [
                        dk_part.reshape(total_keys, head_cols),
                        dv_part.reshape(total_keys, head_cols),
                    ],
                    axis=1,
                ),
            )

        dq_part, kv_part = compute()
        return (dq_sum + dq_part, kv_part)

    dq_sum, kv_grads = lax.fori_loop(
        0,
        group_count,
        add_grads,
        (
            jnp.zeros((tok_rows, HEADS, HEAD), jnp.float32),
            jnp.zeros((total_keys, 2 * head_cols), jnp.float32),
        ),
    )
    summed = lax.psum_scatter(
        rounded(kv_grads).astype(jnp.bfloat16), "seq", scatter_dimension=0, tiled=True
    ).astype(jnp.float32)
    grad_qkv = jnp.concatenate([dq_sum.reshape(tok_rows, head_cols), summed], axis=1).astype(
        jnp.bfloat16
    )
    d_normed = lax.dot_general(
        grad_qkv, w_qkv, (((1,), (1,)), ((), ())), preferred_element_type=jnp.float32
    )
    gained = d_normed * norm_gain
    d_frames = (
        inverse * (gained - unit_rows * jnp.mean(gained * unit_rows, axis=-1, keepdims=True))
    ).astype(jnp.bfloat16)
    w_part = lax.psum_scatter(
        rounded(
            lax.dot_general(
                normed, grad_qkv, (((0,), (0,)), ((), ())), preferred_element_type=jnp.float32
            )
        ).astype(jnp.bfloat16),
        "seq",
        scatter_dimension=0,
        tiled=True,
    )
    w_total = lax.psum(w_part, "dp").astype(jnp.float32)
    w_grad = w_total * (1.0 / math.sqrt(total_keys * lax.axis_size("dp")))
    return (d_frames[None], w_grad)


def solution(mesh):
    return jax.shard_map(
        body,
        mesh=mesh,
        in_specs=(
            P("dp", "seq", None),
            P("dp", "seq"),
            P("dp", None),
            P(),
            P(),
            P("dp", "seq", None),
        ),
        out_specs=(P("dp", "seq", None), P("seq", None)),
        check_vma=False,
    )
```

profile of v0, /device:TPU:1, one launch (start us, length us, event | category | flops | bytes accessed | tf_op | source)
XLA Modules:
  0.0 635.3 jit_solution(11670641613337491043)
XLA Ops:
  8.8 71.3 %all-gather.11.cloned.1.call-done = bf16[1,2048,1024]{2,1,0:T(8,128)(2,1)} async-done(((bf16[1,128,1024]{2,1,0:T(8,128)(2,1)}), bf16[1,2048,1024]{2,1,0:T(8,128)(2,1)}) %all-gather.11.cloned.1.call-update) | async-done | bytes 4194320 | tf_op jit(solution)/shard_map/all_gather | solution.py:38
  80.1 3.8 gather_fusion
  84.1 3.9 convolution_convert_fusion.2
  89.7 25.4 %all-gather.1 = bf16[1,2048]{1,0:T(2,128)(2,1)S(1)} all-gather(bf16[1,128]{1,0:T(2,128)(2,1)S(1)} %convert_element_type.50), channel_id=3, replica_groups=mesh['seq'=16,'dp'=16] {'seq'}, dimensions={1}, use_global_device_ids=true | all-gather | bytes 4352 | tf_op jit(solution)/shard_map/all_gather | solution.py:39
  116.5 24.9 %all-gather.2 = bf16[16,1,128]{2,1,0:T(2,128)(2,1)S(1)} all-gather(bf16[1,1,128]{2,1,0:T(2,128)(2,1)S(1)} %select_bitcast_fusion), channel_id=1, replica_groups=mesh['seq'=16,'dp'=16] {'seq'}, dimensions={0}, use_global_device_ids=true | all-gather | bytes 4352 | tf_op jit(solution)/shard_map/all_gather | solution.py:54
  142.2 21.2 %all-gather.7.cloned.1.call-done = bf16[2048,1024]{1,0:T(8,128)(2,1)} async-done(((bf16[128,1024]{1,0:T(8,128)(2,1)}), bf16[2048,1024]{1,0:T(8,128)(2,1)}) %all-gather.7.cloned.1.call-update) | async-done | bytes 4194320 | tf_op jit(solution)/shard_map/all_gather | solution.py:52
  163.4 6.5 %copy.39 = bf16[2048,1024]{0,1:T(8,128)(2,1)} copy(bf16[2048,1024]{1,0:T(8,128)(2,1)} %all-gather.7.cloned.1.call-done) | data formatting | bytes 8388608 | tf_op jit(solution)/shard_map/while/body/eval_jaxpr/reshape | solution.py:65
  169.9 5.1 fusion.2
  175.0 3.2 copy-done
  178.2 4.5 convolution_convert_fusion.1
  182.8 55.8 %all-gather.9.cloned.1.call-done = bf16[2048,1024]{1,0:T(8,128)(2,1)} async-done(((bf16[128,1024]{1,0:T(8,128)(2,1)}), bf16[2048,1024]{1,0:T(8,128)(2,1)}) %all-gather.9.cloned.1.call-update) | async-done | bytes 4194320 | tf_op jit(solution)/shard_map/all_gather | solution.py:53
  238.5 6.5 %copy.41 = bf16[2048,1024]{0,1:T(8,128)(2,1)} copy(bf16[2048,1024]{1,0:T(8,128)(2,1)} %all-gather.9.cloned.1.call-done) | data formatting | bytes 8388608 | tf_op jit(solution)/shard_map/while/body/eval_jaxpr/reshape | solution.py:66
  245.0 7.3 %fusion.13 = f32[128,8]{0,1:T(8,128)S(1)} fusion(bf16[2048,8,128]{0,2,1:T(8,128)(2,1)} %bitcast.50, bf16[128,8,128]{0,2,1:T(8,128)(2,1)S(1)} %bitcast.59, f32[8,128,2048]{2,1,0:T(8,128)} %copy-done, f32[8,128]{1,0:T(8,128)S(1)} %get-tuple-element.73, pred[128,2048]{1,0:T(8,128)(4,1)S(1)} %compare_and_fusion), kind=kOutput, calls=%fused_computation.20 | convolution fusion | flops 545651712 | bytes 13115392 | tf_op jit(solution)/shard_map/while/body/eval_jaxpr/hqk,khd->qhd/dot_general | solution.py:94
  252.3 5.2 fusion
  257.6 2.0 copy-done.2
  259.5 3.2 multiply_convert_fusion
  262.7 8.3 %pad_maximum_fusion = bf16[2048,2048]{0,1:T(8,128)(2,1)} fusion(bf16[2048,1024]{0,1:T(8,128)(2,1)} %bitcast.52, bf16[2048,1024]{0,1:T(8,128)(2,1)} %bitcast.49), kind=kLoop, calls=%fused_computation.2 | loop fusion | flops 16777216 | bytes 16777216 | tf_op jit(solution)/shard_map/while/body/eval_jaxpr/concatenate | solution.py:132
  271.1 12.2 %copy.37 = bf16[2048,2048]{1,0:T(8,128)(2,1)} copy(bf16[2048,2048]{0,1:T(8,128)(2,1)} %pad_maximum_fusion) | data formatting | bytes 16777216
  283.6 4.7 fusion.12
  288.3 103.2 %reduce-scatter.7.cloned.1.call-done = bf16[128,2048]{1,0:T(8,128)(2,1)} async-done(((bf16[2048,2048]{1,0:T(8,128)(2,1)}), bf16[128,2048]{1,0:T(8,128)(2,1)}) %reduce-scatter.7.cloned.1.call-update) | async-done | bytes 524304
  392.9 4.6 convolution_convert_fusion
  397.6 5.1 fusion.20
  402.7 71.0 %reduce-scatter.5.cloned.1.call-done = bf16[64,3072]{1,0:T(8,128)(2,1)} async-done(((bf16[1024,3072]{1,0:T(8,128)(2,1)}), bf16[64,3072]{1,0:T(8,128)(2,1)}) %reduce-scatter.5.cloned.1.call-update) | async-done | bytes 393232 | tf_op jit(solution)/shard_map/reduce_scatter | solution.py:166
  474.7 151.8 %all-reduce.2.cloned.1.call-done = bf16[64,3072]{1,0:T(8,128)(2,1)} async-done(((bf16[64,3072]{1,0:T(8,128)(2,1)}), bf16[64,3072]{1,0:T(8,128)(2,1)}) %all-reduce.2.cloned.1.call-update) | async-done | bytes 393232 | tf_op jit(solution)/shard_map/psum | solution.py:176
  (44 shorter events, 10.1 us)
Async XLA Ops:
  7.2 72.9 %all-gather.11.cloned.1.call-start = ((), (), s32[]{:S(2)}) async-start(), calls=%async_computation.6 | async-start | bytes 4456448 | tf_op jit(solution)/shard_map/all_gather | solution.py:38
  7.9 155.5 %all-gather.7.cloned.1.call-start = ((), (), s32[]{:S(2)}) async-start(), calls=%async_computation.2 | async-start | bytes 4456448 | tf_op jit(solution)/shard_map/all_gather | solution.py:52
  84.1 5.6 copy-start.5
  84.1 57.4 %copy-start.3 = (bf16[1,128,1024]{2,1,0:T(8,128)(2,1)S(1)}, bf16[1,128,1024]{2,1,0:T(8,128)(2,1)}, u32[]{:S(2)}) copy-start(bf16[1,128,1024]{2,1,0:T(8,128)(2,1)} %param.11) | copy-start | bytes 786436
  88.9 149.6 %all-gather.9.cloned.1.call-start = ((), (), s32[]{:S(2)}) async-start(), calls=%async_computation.3 | async-start | bytes 4456448 | tf_op jit(solution)/shard_map/all_gather | solution.py:53
  89.7 301.9 %reduce-scatter.7.cloned.1.call-start = ((), (), s32[]{:S(2)}) async-start(), calls=%async_computation.7 | async-start | bytes 8912896
  175.0 3.2 copy-start
  245.0 7.3 %copy-start.1 = (f32[8,128,2048]{2,1,0:T(8,128)S(1)}, f32[8,128,2048]{2,1,0:T(8,128)}, u32[]{:S(2)}) copy-start(f32[8,128,2048]{2,1,0:T(8,128)} %copy-done) | copy-start | bytes 25165828
  257.6 2.0 copy-start.2
  283.3 109.6 %copy-start.4 = (f32[1024]{0:T(1024)S(1)}, f32[1024]{0:T(1024)}, u32[]{:S(2)}) copy-start(f32[1024]{0:T(1024)} %param.9) | copy-start | bytes 12292
  283.3 190.4 %reduce-scatter.5.cloned.1.call-start = ((), (), s32[]{:S(2)}) async-start(), calls=%async_computation.4 | async-start | bytes 6684672 | tf_op jit(solution)/shard_map/reduce_scatter | solution.py:166
  397.6 228.9 %all-reduce.2.cloned.1.call-start = ((), (), s32[]{:S(2)}) async-start(), calls=%async_computation.5 | async-start | bytes 786432 | tf_op jit(solution)/shard_map/psum | solution.py:176
Sparse Core Ops, SparseCore 0:
  9.8 70.2 all-gather.10
  89.0 74.2 all-gather.6
  165.7 72.7 all-gather.8
  283.5 108.0 reduce-scatter.6
  397.7 76.0 reduce-scatter.4
  476.2 150.2 all-reduce.1
where the time goes:
time: 636 us; the launch traced here: 635 us
  waiting for transfers between devices  476 us (75%)
  blocking collectives  50.4 us (8%)
  matrix products  43.7 us (7%)
  local copies, waits for them, and re-layouts  38.1 us (6%)
  between operations  14.3 us (2%)
  other arithmetic  12.6 us (2%)
    psum x1, waiting for transfers between devices, body(): w_total = lax.psum(w_part, 'dp').astype(jnp.float32)  152 us
    unnamed x7, waiting for transfers between devices  105 us
    all_gather x1, waiting for transfers between devices, body(): lax.all_gather(frames, 'seq', axis=0, tiled=True)  71.3 us
    reduce_scatter x1, waiting for transfers between devices, body(): lax.psum_scatter(rounded(lax.dot_general(normed, grad_qkv, (((0,), (0,)),...  71 us
    all_gather x1, waiting for transfers between devices, body(): lax.all_gather(projected[:, 2 * head_cols:], 'seq', axis=0, tiled=True)  55.8 us
    all_gather x1, blocking collectives, body(): lax.all_gather(doc_low, 'seq', axis=0, tiled=True)  25.4 us
    all_gather x1, blocking collectives, body(): lax.all_gather(new_docs, 'seq', axis=0, tiled=True)  24.9 us
    all_gather x1, waiting for transfers between devices, body(): lax.all_gather(projected[:, head_cols:2 * head_cols], 'seq', axis=0, tile...  21.2 us
  transfers between devices with their start and end apart: 6, of which 6 were waited for; matrix products, arithmetic and copies ran while one was open for 5% of the time, Pallas kernels for 0%

commit v1 on v0

--- a/solution.py
+++ b/solution.py
@@ -7,6 +7,11 @@
 HEADS = 8
 HEAD = 128
 BLOCK = 128
+
+
+def gather_over(block, name, dim):
+    sent = jnp.stack([block] * lax.axis_size(name))
+    return jnp.concatenate(lax.all_to_all(sent, name, 0, 0), axis=dim)
 
 
 def rounded(value):
@@ -34,10 +39,7 @@
     first_own = my_index * tok_rows
     my_pos = lax.dynamic_slice_in_dim(key_pos, first_own, tok_rows, 0)
     doc_low = doc_ids[0].astype(jnp.bfloat16)
-    pieces = (
-        lax.all_gather(frames, "seq", axis=0, tiled=True),
-        lax.all_gather(doc_low, "seq", axis=0, tiled=True),
-    )
+    pieces = (lax.all_gather(frames, "seq", axis=0, tiled=True), gather_over(doc_low, "seq", 0))
     length = pieces[0].shape[0]
     inside = (my_pos >= 0) & (my_pos < length)
     clipped = jnp.clip(my_pos, 0, length - 1)

time: 636 us -> 636 us (level)
  blocking collectives: 50.4 us -> 24.7 us
  waiting for transfers between devices: 476 us -> 497 us
    all_gather x1 -> x0, blocking collectives: 25.4 us -> none  [body(): lax.all_gather(doc_low, 'seq', axis=0, tiled=True)]
    all_gather x1, waiting for transfers between devices: 21.2 us -> 35 us  [body(): lax.all_gather(projected[:, head_cols:2 * head_cols], 'seq', axis=0, tile...]
    all_to_all x0 -> x1, waiting for transfers between devices: none -> 7.05 us  [gather_over(): return jnp.concatenate(lax.all_to_all(sent, name, 0, 0), axis=dim)]
  transfers between devices with their start and end apart: 6 -> 7, of which waited for: 6 -> 7; matrix products, arithmetic and copies ran while one was open for 5% -> 5% of each run, Pallas kernels for 0% -> 0%
where the time goes in v1:
time: 636 us; the launch traced here: 635 us
  waiting for transfers between devices  497 us (78%)
  matrix products  43.8 us (7%)
  local copies, waits for them, and re-layouts  38.7 us (6%)
  blocking collectives  24.7 us (4%)
  between operations  14.3 us (2%)
  other arithmetic  12.6 us (2%)
    psum x1, waiting for transfers between devices, body(): w_total = lax.psum(w_part, 'dp').astype(jnp.float32)  151 us
    unnamed x7, waiting for transfers between devices  105 us
    reduce_scatter x1, waiting for transfers between devices, body(): lax.psum_scatter(rounded(lax.dot_general(normed, grad_qkv, (((0,), (0,)),...  71.7 us
    all_gather x1, waiting for transfers between devices, body(): lax.all_gather(frames, 'seq', axis=0, tiled=True)  71.3 us
    all_gather x1, waiting for transfers between devices, body(): lax.all_gather(projected[:, 2 * head_cols:], 'seq', axis=0, tiled=True)  56.2 us
    all_gather x1, waiting for transfers between devices, body(): lax.all_gather(projected[:, head_cols:2 * head_cols], 'seq', axis=0, tile...  35 us
    all_gather x1, blocking collectives, body(): lax.all_gather(new_docs, 'seq', axis=0, tiled=True)  24.7 us
    unnamed x15, local copies, waits for them, and re-layouts  18.9 us
  transfers between devices with their start and end apart: 7, of which 7 were waited for; matrix products, arithmetic and copies ran while one was open for 5% of the time, Pallas kernels for 0%

profile of v1, /device:TPU:1, one launch (start us, length us, event | category | flops | bytes accessed | tf_op | source)
XLA Modules:
  0.0 635.2 jit_solution(13368393092581142258)
XLA Ops:
  8.8 71.3 %all-gather.10.cloned.1.call-done = bf16[1,2048,1024]{2,1,0:T(8,128)(2,1)} async-done(((bf16[1,128,1024]{2,1,0:T(8,128)(2,1)}), bf16[1,2048,1024]{2,1,0:T(8,128)(2,1)}) %all-gather.10.cloned.1.call-update) | async-done | bytes 4194320 | tf_op jit(solution)/shard_map/all_gather | solution.py:42
  80.1 3.8 gather_fusion
  84.1 3.9 convolution_convert_fusion.2
  90.3 3.5 all-to-all-start
  94.0 7.0 %all-to-all-done = bf16[16,1,128]{2,1,0:T(2,128)(2,1)S(1)} async-done(((bf16[16,1,128]{2,1,0:T(2,128)(2,1)}), bf16[16,1,128]{2,1,0:T(2,128)(2,1)S(1)}, u32[]{:S(2)}, u32[]{:S(2)}) %all-to-all-start) | async-done | bytes 4128 | tf_op jit(solution)/shard_map/all_to_all | solution.py:14
  102.4 24.7 %all-gather.1 = bf16[16,1,128]{2,1,0:T(2,128)(2,1)S(1)} all-gather(bf16[1,1,128]{2,1,0:T(2,128)(2,1)S(1)} %select_bitcast_fusion), channel_id=1, replica_groups=mesh['seq'=16,'dp'=16] {'seq'}, dimensions={0}, use_global_device_ids=true | all-gather | bytes 4352 | tf_op jit(solution)/shard_map/all_gather | solution.py:56
  127.6 35.0 %all-gather.6.cloned.1.call-done = bf16[2048,1024]{1,0:T(8,128)(2,1)} async-done(((bf16[128,1024]{1,0:T(8,128)(2,1)}), bf16[2048,1024]{1,0:T(8,128)(2,1)}) %all-gather.6.cloned.1.call-update) | async-done | bytes 4194320 | tf_op jit(solution)/shard_map/all_gather | solution.py:54
  162.6 6.5 %copy.39 = bf16[2048,1024]{0,1:T(8,128)(2,1)} copy(bf16[2048,1024]{1,0:T(8,128)(2,1)} %all-gather.6.cloned.1.call-done) | data formatting | bytes 8388608 | tf_op jit(solution)/shard_map/while/body/eval_jaxpr/reshape | solution.py:67
  169.1 5.1 fusion.2
  174.3 3.2 copy-done
  177.4 4.6 convolution_convert_fusion.1
  182.0 56.2 %all-gather.8.cloned.1.call-done = bf16[2048,1024]{1,0:T(8,128)(2,1)} async-done(((bf16[128,1024]{1,0:T(8,128)(2,1)}), bf16[2048,1024]{1,0:T(8,128)(2,1)}) %all-gather.8.cloned.1.call-update) | async-done | bytes 4194320 | tf_op jit(solution)/shard_map/all_gather | solution.py:55
  238.3 6.5 %copy.41 = bf16[2048,1024]{0,1:T(8,128)(2,1)} copy(bf16[2048,1024]{1,0:T(8,128)(2,1)} %all-gather.8.cloned.1.call-done) | data formatting | bytes 8388608 | tf_op jit(solution)/shard_map/while/body/eval_jaxpr/reshape | solution.py:68
  244.8 7.3 %fusion.13 = f32[128,8]{0,1:T(8,128)S(1)} fusion(bf16[2048,8,128]{0,2,1:T(8,128)(2,1)} %bitcast.54, bf16[128,8,128]{0,2,1:T(8,128)(2,1)S(1)} %bitcast.63, f32[8,128,2048]{2,1,0:T(8,128)} %copy-done, f32[8,128]{1,0:T(8,128)S(1)} %get-tuple-element.73, pred[128,2048]{1,0:T(8,128)(4,1)S(1)} %compare_and_fusion), kind=kOutput, calls=%fused_computation.20 | convolution fusion | flops 545651712 | bytes 13115392 | tf_op jit(solution)/shard_map/while/body/eval_jaxpr/hqk,khd->qhd/dot_general | solution.py:96
  252.1 5.2 fusion
  259.3 3.2 multiply_convert_fusion
  262.5 8.4 %pad_maximum_fusion = bf16[2048,2048]{0,1:T(8,128)(2,1)} fusion(bf16[2048,1024]{0,1:T(8,128)(2,1)} %bitcast.56, bf16[2048,1024]{0,1:T(8,128)(2,1)} %bitcast.53), kind=kLoop, calls=%fused_computation.2 | loop fusion | flops 16777216 | bytes 16777216 | tf_op jit(solution)/shard_map/while/body/eval_jaxpr/concatenate | solution.py:134
  270.8 12.2 %copy.37 = bf16[2048,2048]{1,0:T(8,128)(2,1)} copy(bf16[2048,2048]{0,1:T(8,128)(2,1)} %pad_maximum_fusion) | data formatting | bytes 16777216
  283.4 4.7 fusion.12
  288.1 103.5 %reduce-scatter.7.cloned.1.call-done = bf16[128,2048]{1,0:T(8,128)(2,1)} async-done(((bf16[2048,2048]{1,0:T(8,128)(2,1)}), bf16[128,2048]{1,0:T(8,128)(2,1)}) %reduce-scatter.7.cloned.1.call-update) | async-done | bytes 524304
  392.9 4.6 convolution_convert_fusion
  397.6 5.1 fusion.20
  402.7 71.7 %reduce-scatter.5.cloned.1.call-done = bf16[64,3072]{1,0:T(8,128)(2,1)} async-done(((bf16[1024,3072]{1,0:T(8,128)(2,1)}), bf16[64,3072]{1,0:T(8,128)(2,1)}) %reduce-scatter.5.cloned.1.call-update) | async-done | bytes 393232 | tf_op jit(solution)/shard_map/reduce_scatter | solution.py:168
  475.4 151.0 %all-reduce.2.cloned.1.call-done = bf16[64,3072]{1,0:T(8,128)(2,1)} async-done(((bf16[64,3072]{1,0:T(8,128)(2,1)}), bf16[64,3072]{1,0:T(8,128)(2,1)}) %all-reduce.2.cloned.1.call-update) | async-done | bytes 393232 | tf_op jit(solution)/shard_map/psum | solution.py:178
  (46 shorter events, 12.6 us)
Async XLA Ops:
  7.2 72.9 %all-gather.10.cloned.1.call-start = ((), (), s32[]{:S(2)}) async-start(), calls=%async_computation.7 | async-start | bytes 4456448 | tf_op jit(solution)/shard_map/all_gather | solution.py:42
  7.9 154.7 %all-gather.6.cloned.1.call-start = ((), (), s32[]{:S(2)}) async-start(), calls=%async_computation.3 | async-start | bytes 4456448 | tf_op jit(solution)/shard_map/all_gather | solution.py:54
  84.1 5.6 copy-start.5
  84.1 9.8 %copy-start.3 = (bf16[1,128,1024]{2,1,0:T(8,128)(2,1)S(1)}, bf16[1,128,1024]{2,1,0:T(8,128)(2,1)}, u32[]{:S(2)}) copy-start(bf16[1,128,1024]{2,1,0:T(8,128)(2,1)} %param.11) | copy-start | bytes 786436
  88.9 149.3 %all-gather.8.cloned.1.call-start = ((), (), s32[]{:S(2)}) async-start(), calls=%async_computation.4 | async-start | bytes 4456448 | tf_op jit(solution)/shard_map/all_gather | solution.py:55
  90.3 10.8 %all-to-all-start = ((bf16[16,1,128]{2,1,0:T(2,128)(2,1)}), bf16[16,1,128]{2,1,0:T(2,128)(2,1)S(1)}, u32[]{:S(2)}, u32[]{:S(2)}) async-start(bf16[16,1,128]{2,1,0:T(2,128)(2,1)} %stack.2), calls=%async_computation | async-start | bytes 16384 | tf_op jit(solution)/shard_map/all_to_all | solution.py:14
  93.8 297.8 %reduce-scatter.7.cloned.1.call-start = ((), (), s32[]{:S(2)}) async-start(), calls=%async_computation.8 | async-start | bytes 8912896
  174.2 3.2 copy-start
  244.8 7.3 %copy-start.1 = (f32[8,128,2048]{2,1,0:T(8,128)S(1)}, f32[8,128,2048]{2,1,0:T(8,128)}, u32[]{:S(2)}) copy-start(f32[8,128,2048]{2,1,0:T(8,128)} %copy-done) | copy-start | bytes 25165828
  257.3 2.0 copy-start.2
  283.1 109.8 %copy-start.4 = (f32[1024]{0:T(1024)S(1)}, f32[1024]{0:T(1024)}, u32[]{:S(2)}) copy-start(f32[1024]{0:T(1024)} %param.9) | copy-start | bytes 12292
  283.1 191.3 %reduce-scatter.5.cloned.1.call-start = ((), (), s32[]{:S(2)}) async-start(), calls=%async_computation.5 | async-start | bytes 6684672 | tf_op jit(solution)/shard_map/reduce_scatter | solution.py:168
  397.6 228.9 %all-reduce.2.cloned.1.call-start = ((), (), s32[]{:S(2)}) async-start(), calls=%async_computation.6 | async-start | bytes 786432 | tf_op jit(solution)/shard_map/psum | solution.py:178
Sparse Core Ops, SparseCore 0:
  9.8 70.2 all-gather.9
  89.0 73.5 all-gather.5
  165.0 73.2 all-gather.7
  283.2 108.3 reduce-scatter.6
  397.7 76.6 reduce-scatter.4
  476.9 149.4 all-reduce.1
